TPU v7x, 128 devices: a whole 4x4x4 slice. The times are simulated.
128 devices in a mesh: rep: 16 (over y, x_lo, core), blk: 8 (over z, x_hi).
Axes of the slice: x: 4 (x_hi: 2, x_lo: 2; x = x_hi * 2 + x_lo), y: 4, z: 4, core: 2. Of those that a mesh axis runs over, the one named last changes fastest.
Arguments:
- tokens: bfloat16 [16384, 1536], P(('rep', 'blk')), may hold values from -64 to 64
- attn_in: float32 [1536, 2048], P(('rep', 'blk')), may hold values from -8 to 8
- attn_out: float32 [1536, 1536], P(('rep', 'blk')), may hold values from -0.15625 to 0.15625
- expert_in: float32 [16, 1536, 1536], P(None, ('rep', 'blk')), may hold values from -0.15625 to 0.15625
- expert_out: float32 [16, 768, 1536], P(None, ('rep', 'blk')), may hold values from -0.21875 to 0.21875
- attn_gain: float32 [1536], replicated, may hold values from 0.25 to 1.75
- moe_gain: float32 [1536], replicated, may hold values from 0.25 to 1.75
- lengths: int32 [16, 6], P('rep'), may hold values from 1 to 512, 1024 in all within a row
- page_table: int32 [16, 8], P('rep'), may hold values from 0 to 7, each once within a row
- routes: int32 [16384, 4], P(('rep', 'blk')), may hold values from 0 to 15, all different within a row; in each aligned block of 128 rows (0 to 127, 128 to 255, ...) at most 64 rows name the same one
- gates: bfloat16 [16384, 4], P(('rep', 'blk')), may hold values from 0.19921875 to 1
Outputs:
- mixed: bfloat16 [16384, 1536], P(('rep', 'blk'))
- kv_cache: bfloat16 [128, 128, 512], P(('rep', 'blk'))
Inputs may be any that keep to these rules, and one draw needn't show every extreme that they name: Each replica's lengths sum to 1024. `page_table`: each replica's row is a permutation of its 8 pages. `routes`: a token names 4 different experts; among the rows of one device no expert is named more than 64 times.
All inputs are finite; a program needn't handle non-finite values.
Results may differ from a plain program's by a relative error of at most 0.013.
Values may be sent and summed in bfloat16 or wider, within the bound.
A program may use at most 128 MiB of HBM per device.

v0:
```python
import functools
import math
import jax
import jax.numpy as jnp
from jax import lax
from jax.sharding import PartitionSpec as P

D = 1536
FF = 768
QH = 12
KVH = 2
HD = 128
E = 16
PAGE = 128
CAP = 64
QW = 1536


def rms_scale(values, gain):
    values = values.astype(jnp.float32)
    mean_sq = jnp.mean(values * values, axis=-1, keepdims=True)
    return values * lax.rsqrt(mean_sq + 1e-06) * gain


def rotate(values, position):
    half = values.shape[-1] // 2
    steps_all = jnp.arange(half, dtype=jnp.float32)
    frequency = jnp.exp(steps_all * (-2.0 * math.log(10000.0) / values.shape[-1]))
    angle = position[:, None] * frequency[None, :]
    cosine = jnp.cos(angle)[:, None, :]
    sine = jnp.sin(angle)[:, None, :]
    front = values[..., :half]
    behind = values[..., half:]
    return jnp.concatenate(
        [front * cosine - behind * sine, behind * cosine + front * sine], axis=-1
    )


def segment_info(lengths, count):
    starts = jnp.cumsum(lengths) - lengths
    index = jnp.arange(count, dtype=jnp.int32)
    member = (index[:, None] >= starts[None, :]).astype(jnp.int32)
    segment = jnp.sum(member, axis=1) - 1
    owner = segment[:, None] == jnp.arange(lengths.shape[0], dtype=jnp.int32)[None, :]
    begin = jnp.sum(jnp.where(owner, starts[None, :], 0), axis=1)
    return (segment, index - begin)


def slot_tables(weight, depth):
    member = (weight > 0).astype(jnp.int32)
    ranked = jnp.cumsum(member, axis=0) - 1
    slot_ids = jnp.arange(depth, dtype=jnp.int32)
    hit = (member.T[:, None, :] == 1) & (ranked.T[:, None, :] == slot_ids[None, :, None])
    onehot = hit.astype(jnp.bfloat16)
    gated = jnp.where(hit, weight.T[:, None, :], jnp.zeros((), jnp.bfloat16))
    return (onehot, gated)


def body(
    tokens,
    attn_in,
    attn_out,
    expert_in,
    expert_out,
    attn_gain,
    moe_gain,
    lengths,
    page_table,
    routes,
    gates,
):
    count = tokens.shape[0]
    cycle_size = lax.axis_size("blk")
    place = lax.axis_index("blk")
    group_rows = count * cycle_size
    local_experts = E // cycle_size
    heads_per = QH // KVH
    segment_all, position_all = segment_info(lengths[0], group_rows)
    first = place * count
    my_index = first + jnp.arange(count, dtype=jnp.int32)
    my_segment = lax.dynamic_slice_in_dim(segment_all, first, count)
    my_position = lax.dynamic_slice_in_dim(position_all, first, count).astype(jnp.float32)
    normed = rms_scale(tokens, attn_gain).astype(jnp.bfloat16)
    columns = normed
    projected = jnp.dot(
        columns,
        lax.all_gather(attn_in.astype(jnp.bfloat16), ("rep", "blk"), axis=0, tiled=True),
        preferred_element_type=jnp.float32,
    )
    queries = rotate(projected[:, :QW].reshape(count, QH, HD), my_position).astype(jnp.bfloat16)
    keys_here = rotate(
        projected[:, QW : QW + KVH * HD].reshape(count, KVH, HD), my_position
    ).astype(jnp.bfloat16)
    values_here = projected[:, QW + KVH * HD :].astype(jnp.bfloat16)
    cache_here = jnp.concatenate([keys_here.reshape(count, KVH * HD), values_here], axis=1)
    cache_all = lax.all_gather(cache_here, "blk", axis=0, tiled=True)
    keys_all = cache_all[:, : KVH * HD].reshape(group_rows, KVH, HD)
    values_all = cache_all[:, KVH * HD :].reshape(group_rows, KVH, HD)
    grouped = queries.reshape(count, KVH, heads_per, HD)
    scores = jnp.einsum(
        "igrd,jgd->grij", grouped, keys_all, preferred_element_type=jnp.float32
    ) / math.sqrt(HD)
    key_index = jnp.arange(group_rows, dtype=jnp.int32)
    allowed = (my_segment[:, None] == segment_all[None, :]) & (
        key_index[None, :] <= my_index[:, None]
    )
    scores = jnp.where(allowed[None, None], scores, jnp.float32(-1e30))
    highest = jnp.max(scores, axis=-1, keepdims=True)
    weights = jnp.exp(scores - highest)
    probs = (weights / jnp.sum(weights, axis=-1, keepdims=True)).astype(jnp.bfloat16)
    attended = jnp.einsum("grij,jgd->igrd", probs, values_all, preferred_element_type=jnp.float32)
    attended = attended.astype(jnp.bfloat16).reshape(count, QW)
    columns = attended
    hidden = tokens.astype(jnp.float32) + jnp.dot(
        columns,
        lax.all_gather(attn_out.astype(jnp.bfloat16), ("rep", "blk"), axis=0, tiled=True),
        preferred_element_type=jnp.float32,
    )
    page_count = count // PAGE
    targets = place * page_count + jnp.arange(page_count, dtype=jnp.int32)
    table = page_table[0]
    logical = jnp.sum(
        jnp.where(
            table[None, :] == targets[:, None],
            jnp.arange(table.shape[0], dtype=jnp.int32)[None, :],
            0,
        ),
        axis=1,
    )
    row_ids = logical[:, None] * PAGE + jnp.arange(PAGE, dtype=jnp.int32)[None, :]
    kv_pages = cache_all[row_ids]
    normed_two = rms_scale(hidden, moe_gain).astype(jnp.bfloat16)
    expert_ids = jnp.arange(E, dtype=jnp.int32)
    dense = jnp.sum(
        jnp.where(
            routes[:, :, None] == expert_ids[None, None, :],
            gates.astype(jnp.float32)[:, :, None],
            jnp.float32(0.0),
        ),
        axis=1,
    ).astype(jnp.bfloat16)
    owned_in, owned_out = (
        lax.all_to_all(
            expert_in.astype(jnp.bfloat16), "blk", split_axis=0, concat_axis=1, tiled=True
        ),
        lax.all_to_all(
            expert_out.astype(jnp.bfloat16), "blk", split_axis=0, concat_axis=1, tiled=True
        ),
    )
    rows_all, weight_all = (
        lax.all_gather(normed_two, "blk", axis=0, tiled=True),
        lax.all_gather(dense, "blk", axis=0, tiled=True),
    )
    owned_weight = lax.dynamic_slice_in_dim(weight_all, place * local_experts, local_experts, 1)
    owned_weight = owned_weight.reshape(cycle_size, count, local_experts)
    onehot, gated = jax.vmap(functools.partial(slot_tables, depth=CAP), in_axes=0, out_axes=1)(
        owned_weight
    )
    chosen = jnp.einsum(
        "jsct,stm->jscm",
        onehot,
        rows_all.reshape(cycle_size, count, D),
        preferred_element_type=jnp.float32,
    ).astype(jnp.bfloat16)
    run_chosen = chosen.reshape(local_experts, cycle_size * CAP, D)
    section = run_chosen
    gate_up = jnp.einsum(
        "erd,edf->erf",
        section,
        lax.all_gather(owned_in, "rep", axis=1, tiled=True),
        preferred_element_type=jnp.float32,
    )
    activated = (jax.nn.relu(gate_up[..., :FF]) * gate_up[..., FF:]).astype(jnp.bfloat16)
    section = activated
    summed = jnp.einsum(
        "erf,efd->erd",
        section,
        lax.all_gather(owned_out, "rep", axis=1, tiled=True),
        preferred_element_type=jnp.float32,
    )
    results = summed.astype(jnp.bfloat16)
    results = results.reshape(local_experts, cycle_size, CAP, D)
    summed = jnp.einsum("jsct,jscm->stm", gated, results, preferred_element_type=jnp.float32)
    expert_term = lax.psum_scatter(
        summed.reshape(count * lax.axis_size("blk"), D).astype(jnp.bfloat16),
        "blk",
        scatter_dimension=0,
        tiled=True,
    ).astype(jnp.float32)
    mixed = (hidden + expert_term).astype(jnp.bfloat16)
    return (mixed, kv_pages)


def solution(mesh):
    in_specs = (
        P(("rep", "blk"), None),
        P(("rep", "blk"), None),
        P(("rep", "blk"), None),
        P(None, ("rep", "blk"), None),
        P(None, ("rep", "blk"), None),
        P(),
        P(),
        P("rep", None),
        P("rep", None),
        P(("rep", "blk"), None),
        P(("rep", "blk"), None),
    )
    out_specs = (P(("rep", "blk"), None), P(("rep", "blk"), None, None))
    return jax.shard_map(body, mesh=mesh, in_specs=in_specs, out_specs=out_specs, check_vma=False)
```

profile of v0, /device:TPU:0, one launch (start us, length us, event | category | flops | bytes accessed | tf_op | source)
XLA Modules:
  0.0 961.2 jit_solution(10468634201662940801)
XLA Ops:
  7.2 1.5 convert_bitcast_fusion
  8.8 0.0 all-gather.19.cloned.1.call-start
  8.8 1.5 convert_bitcast_fusion.1
  10.4 0.0 all-gather.9.cloned.1.call-start
  10.4 0.8 reduce-window_clone.1
  11.3 0.7 subtract_bitcast_fusion
  11.9 0.1 convert_reduce_fusion
  12.0 0.1 select_reduce_fusion.1
  12.1 0.1 dynamic-slice_convert_fusion
  12.2 0.2 multiply_cosine_fusion
  12.4 0.1 copy.88
  12.5 0.1 copy.89
  12.6 1.2 fusion.12
  13.8 310.3 %all-gather.17.cloned.1.call-done = bf16[128,12,2048]{2,1,0:T(8,128)(2,1)} async-done(((bf16[1,12,2048]{2,1,0:T(8,128)(2,1)}), bf16[128,12,2048]{2,1,0:T(8,128)(2,1)}) %all-gather.17.cloned.1.call-update) | async-done | bytes 6291472 | tf_op jit(solution)/shard_map/all_gather | solution.py:87
  324.1 10.7 %reshape.228 = bf16[1536,2048]{1,0:T(8,128)(2,1)} reshape(bf16[128,12,2048]{2,1,0:T(8,128)(2,1)} %all-gather.17.cloned.1.call-done) | data formatting | bytes 12582912
  334.8 3.8 fusion.28
  338.7 0.1 reshape.210
  338.7 0.3 subtract_convert_fusion.1
  339.0 0.2 pad_maximum_fusion.2
  339.2 0.7 pad_maximum_fusion.1
  340.0 0.1 dynamic_slice.10
  340.1 0.2 fusion.17
  340.3 297.8 %all-gather.19.cloned.1.call-done = bf16[128,12,1536]{2,1,0:T(8,128)(2,1)} async-done(((bf16[1,12,1536]{2,1,0:T(8,128)(2,1)}), bf16[128,12,1536]{2,1,0:T(8,128)(2,1)}) %all-gather.19.cloned.1.call-update) | async-done | bytes 4718608 | tf_op jit(solution)/shard_map/all_gather | solution.py:116
  638.1 8.2 reshape.230
  646.3 0.1 slice.53
  646.4 0.3 copy.90
  646.6 0.1 subtract_convert_fusion
  646.8 0.2 copy.91
  647.0 0.2 copy.92
  647.2 42.0 %all-gather.9.cloned.1.call-done = bf16[1024,512]{1,0:T(8,128)(2,1)} async-done(((bf16[128,512]{1,0:T(8,128)(2,1)}), bf16[1024,512]{1,0:T(8,128)(2,1)}) %all-gather.9.cloned.1.call-update) | async-done | bytes 1048592 | tf_op jit(solution)/shard_map/all_gather | solution.py:96
  689.3 1.3 fusion.49
  690.5 0.1 reshape.212
  690.7 0.2 copy.113
  690.9 4.8 fusion.50
  695.7 3.5 fusion.11
  699.3 0.4 slice-done.1
  699.7 0.9 multiply_reduce_fusion
  700.6 0.9 copy-done
  701.5 0.9 multiply_convert_fusion
  702.5 0.1 convert_element_type.95
  702.6 0.3 copy.101
  702.9 18.1 %all_to_all.36 = bf16[16,12,1536]{2,1,0:T(8,128)(2,1)S(1)} all-to-all(bf16[16,12,1536]{2,1,0:T(8,128)(2,1)S(1)} %copy.101), channel_id=1, replica_groups=mesh['rep'=16,'blk'=8] {'blk'}, dimensions={0} | all-to-all | bytes 1179648 | tf_op jit(solution)/shard_map/all_to_all | solution.py:143
  721.0 0.6 copy.102
  721.6 0.9 copy.103
  722.6 0.2 copy.104
  722.8 12.0 %all_to_all.37 = bf16[16,6,1536]{2,1,0:T(8,128)(2,1)S(1)} all-to-all(bf16[16,6,1536]{2,1,0:T(8,128)(2,1)S(1)} %copy.104), channel_id=1, replica_groups=mesh['rep'=16,'blk'=8] {'blk'}, dimensions={0} | all-to-all | bytes 589824 | tf_op jit(solution)/shard_map/all_to_all | solution.py:146
  734.8 0.2 copy.105
  735.0 0.8 copy.106
  735.8 0.0 reduce-scatter.2.cloned.1.call-start
  735.9 30.8 %all_gather.24 = bf16[1024,16]{0,1:T(8,128)(2,1)S(1)} all-gather(bf16[128,16]{0,1:T(8,128)(2,1)S(1)} %select_reduce_fusion), channel_id=1, replica_groups=mesh['rep'=16,'blk'=8] {'blk'}, dimensions={0}, use_global_device_ids=true | all-gather | bytes 36864 | tf_op jit(solution)/shard_map/all_gather | solution.py:152
  766.8 0.3 copy.97
  767.0 23.4 %add_bitcast_fusion = s32[2,8,128]{0,1,2:T(8,128)S(1)} fusion(s32[8,128,2]{2,0,1:T(8,128)S(1)} %copy.97), kind=kOutput, calls=%fused_computation.31 | output fusion | flops 262144 | bytes 16384 | tf_op jit(solution)/shard_map/vmap(jit(cumsum))/reduce_window_sum | solution.py:51
  790.4 0.2 copy.98
  790.7 2.9 fusion.2
  793.6 0.3 copy.100
  793.9 28.5 %all-gather.13.cloned.1.call-done = bf16[2,1536,1536]{2,1,0:T(8,128)(2,1)} async-done(((bf16[2,96,1536]{2,1,0:T(8,128)(2,1)}), bf16[2,1536,1536]{2,1,0:T(8,128)(2,1)}) %all-gather.13.cloned.1.call-update) | async-done | bytes 9437200 | tf_op jit(solution)/shard_map/all_gather | solution.py:170
  822.4 10.6 %fusion.55 = f32[2,512,1536]{2,1,0:T(8,128)} fusion(bf16[2,512,1536]{2,1,0:T(8,128)(2,1)S(1)} %bitcast.83, bf16[2,1536,1536]{2,1,0:T(8,128)(2,1)} %all-gather.13.cloned.1.call-done), kind=kOutput, calls=%fused_computation.92 | convolution fusion | flops 4831838208 | bytes 18874368 | tf_op jit(solution)/shard_map/erd,edf->erf/dot_general | solution.py:167
  833.0 30.3 %all-gather.15.cloned.1.call-done = bf16[2,768,1536]{2,1,0:T(8,128)(2,1)} async-done(((bf16[2,48,1536]{2,1,0:T(8,128)(2,1)}), bf16[2,768,1536]{2,1,0:T(8,128)(2,1)}) %all-gather.15.cloned.1.call-update) | async-done | bytes 4718608 | tf_op jit(solution)/shard_map/all_gather | solution.py:178
  863.2 6.8 convolution_convert_fusion
  870.1 2.7 bitcast_convert_fusion
  872.8 0.6 fusion.39
  874.1 1.5 gather_fusion
  875.6 76.9 %reduce-scatter.2.cloned.1.call-done = bf16[128,1536]{1,0:T(8,128)(2,1)} async-done(((bf16[1024,1536]{1,0:T(8,128)(2,1)}), bf16[128,1536]{1,0:T(8,128)(2,1)}) %reduce-scatter.2.cloned.1.call-update) | async-done | bytes 393232 | tf_op jit(solution)/shard_map/reduce_scatter | solution.py:184
  952.5 1.8 add_convert_fusion
  (56 shorter events, 0.5 us)
Async XLA Ops:
  7.2 316.9 %all-gather.17.cloned.1.call-start = ((), (), s32[]{:S(2)}) async-start(), calls=%async_computation.8 | async-start | bytes 8454144 | tf_op jit(solution)/shard_map/all_gather | solution.py:87
  8.8 629.3 %all-gather.19.cloned.1.call-start = ((), (), s32[]{:S(2)}) async-start(), calls=%async_computation.9 | async-start | bytes 6340608 | tf_op jit(solution)/shard_map/all_gather | solution.py:116
  10.4 678.9 %all-gather.9.cloned.1.call-start = ((), (), s32[]{:S(2)}) async-start(), calls=%async_computation.3 | async-start | bytes 1179648 | tf_op jit(solution)/shard_map/all_gather | solution.py:96
  13.8 321.0 %copy-start.3 = (bf16[128,1536]{1,0:T(8,128)(2,1)S(1)}, bf16[128,1536]{1,0:T(8,128)(2,1)}, u32[]{:S(2)}) copy-start(bf16[128,1536]{1,0:T(8,128)(2,1)} %param.11) | copy-start | bytes 1179652
  13.8 321.0 %copy-start.6 = (f32[1536]{0:T(1024)S(1)}, f32[1536]{0:T(1024)}, u32[]{:S(2)}) copy-start(f32[1536]{0:T(1024)} %param.16) | copy-start | bytes 18436
  339.9 450.7 %all-gather.11.cloned.1.call-start = ((), (), s32[]{:S(2)}) async-start(), calls=%async_computation.4 | async-start | bytes 3538944 | tf_op jit(solution)/shard_map/all_gather | solution.py:151
  690.9 8.4 slice-start
  695.7 4.0 slice-start.1
  699.2 2.3 copy-start.7
  699.2 3.2 copy-start.4
  700.6 0.9 copy-start
  701.5 21.1 %copy-start.5 = (f32[16,6,1536]{2,0,1:T(8,128)S(1)}, f32[16,6,1536]{2,0,1:T(8,128)}, u32[]{:S(2)}) copy-start(f32[16,6,1536]{2,0,1:T(8,128)} %param.15) | copy-start | bytes 1769476
  702.4 120.0 %all-gather.13.cloned.1.call-start = ((), (), s32[]{:S(2)}) async-start(), calls=%async_computation.5 | async-start | bytes 10027008 | tf_op jit(solution)/shard_map/all_gather | solution.py:170
  702.5 33.3 %copy-start.9 = (bf16[128,4]{0,1:T(4,128)(2,1)S(1)}, bf16[128,4]{0,1:T(4,128)(2,1)}, u32[]{:S(2)}) copy-start(bf16[128,4]{0,1:T(4,128)(2,1)} %param.21) | copy-start | bytes 3076
  702.6 33.3 %copy-start.8 = (s32[128,4]{0,1:T(4,128)S(1)}, s32[128,4]{0,1:T(4,128)}, u32[]{:S(2)}) copy-start(s32[128,4]{0,1:T(4,128)} %param.20) | copy-start | bytes 6148
  722.5 140.7 %all-gather.15.cloned.1.call-start = ((), (), s32[]{:S(2)}) async-start(), calls=%async_computation.6 | async-start | bytes 5013504 | tf_op jit(solution)/shard_map/all_gather | solution.py:178
  735.8 216.7 %reduce-scatter.2.cloned.1.call-start = ((), (), s32[]{:S(2)}) async-start(), calls=%async_computation.7 | async-start | bytes 3538944 | tf_op jit(solution)/shard_map/reduce_scatter | solution.py:184
  870.1 2.7 copy-start.10
  870.1 4.0 copy-start.2
  870.1 82.4 %copy-start.1 = (f32[128,1536]{1,0:T(8,128)S(1)}, f32[128,1536]{1,0:T(8,128)}, u32[]{:S(2)}) copy-start(f32[128,1536]{1,0:T(8,128)} %copy-done) | copy-start | bytes 2359300
Sparse Core Ops, SparseCore 0:
  10.3 313.7 all-gather.16
  326.3 311.7 all-gather.18
  641.0 48.1 all-gather.8
  702.5 63.4 all-gather.10
  767.5 54.7 all-gather.12
  823.9 39.3 all-gather.14
  872.9 79.5 reduce-scatter.1
where the time goes:
time: 962 us; the launch traced here: 961 us
  waiting for transfers between devices  786 us (82%)
  blocking collectives  60.9 us (6%)
  matrix products  36 us (4%)
  other arithmetic  34.5 us (4%)
  local copies, waits for them, and re-layouts  28.3 us (3%)
  between operations  15.2 us (2%)
    all_gather x1, waiting for transfers between devices, body(): lax.all_gather(attn_in.astype(jnp.bfloat16), ('rep', 'blk'), axis=0, tile...  310 us
    all_gather x1, waiting for transfers between devices, body(): lax.all_gather(attn_out.astype(jnp.bfloat16), ('rep', 'blk'), axis=0, til...  298 us
    reduce_scatter x1, waiting for transfers between devices, body(): lax.psum_scatter(summed.reshape(count * lax.axis_size('blk'), D).astype(j...  76.9 us
    all_gather x1, waiting for transfers between devices, body(): cache_all = lax.all_gather(cache_here, 'blk', axis=0, tiled=True)  42 us
    all_gather x1, blocking collectives, body(): lax.all_gather(dense, 'blk', axis=0, tiled=True)  30.8 us
    all_gather x1, waiting for transfers between devices, body(): lax.all_gather(owned_out, 'rep', axis=1, tiled=True)  30.3 us
    all_gather x1, waiting for transfers between devices, body(): lax.all_gather(owned_in, 'rep', axis=1, tiled=True)  28.5 us
    another operation x1, other arithmetic, slot_tables(): ranked = jnp.cumsum(member, axis=0) - 1  23.4 us
  transfers between devices with their start and end apart: 7, of which 6 were waited for; matrix products, arithmetic and copies ran while one was open for 8% of the time, Pallas kernels for 0%

commit v1 on v0

--- a/solution.py
+++ b/solution.py
@@ -14,6 +14,13 @@
 PAGE = 128
 CAP = 64
 QW = 1536
+
+
+def state_make(mat, row_axis):
+    newest = jnp.stack([mat for _ in range(lax.psum(1, axis_name=row_axis))], 0)
+    return jnp.concatenate(
+        lax.all_to_all(newest, axis_name=row_axis, split_axis=0, concat_axis=0), 1
+    )
 
 
 def rms_scale(values, gain):
@@ -165,10 +172,7 @@
     run_chosen = chosen.reshape(local_experts, cycle_size * CAP, D)
     section = run_chosen
     gate_up = jnp.einsum(
-        "erd,edf->erf",
-        section,
-        lax.all_gather(owned_in, "rep", axis=1, tiled=True),
-        preferred_element_type=jnp.float32,
+        "erd,edf->erf", section, state_make(owned_in, "rep"), preferred_element_type=jnp.float32
     )
     activated = (jax.nn.relu(gate_up[..., :FF]) * gate_up[..., FF:]).astype(jnp.bfloat16)
     section = activated

time: 962 us -> 1060 us (1.10)
  blocking collectives: 60.9 us -> 158 us
  waiting for transfers between devices: 786 us -> 762 us
  local copies, waits for them, and re-layouts: 28.3 us -> 42.6 us
  starting transfers between devices: 0.29 us -> 12.4 us
    all_gather x1, blocking collectives: 30.8 us -> 158 us  [body(): lax.all_gather(dense, 'blk', axis=0, tiled=True)]
    all_gather x1, waiting for transfers between devices: 30.3 us -> 0.01 us  [body(): lax.all_gather(owned_out, 'rep', axis=1, tiled=True)]
    all_to_all x2 -> x0, blocking collectives: 30.1 us -> none  [the longest x1 18.1 us: body(): lax.all_to_all(expert_in.astype(jnp.bfloat16), 'blk', split_axis=0, conca...]
    all_gather x1 -> x0, waiting for transfers between devices: 28.5 us -> none  [body(): lax.all_gather(owned_in, 'rep', axis=1, tiled=True)]
    all_to_all x0 -> x3, waiting for transfers between devices: none -> 25.2 us  [the longest x1 16.5 us: body(): lax.all_to_all(expert_in.astype(jnp.bfloat16), 'blk', split_axis=0, conca...]
    all_to_all x0 -> x3, starting transfers between devices: none -> 12.1 us  [the longest x1 4.92 us: state_make(): lax.all_to_all(newest, axis_name=row_axis, split_axis=0, concat_axis=0)]
  transfers between devices with their start and end apart: 7 -> 9, of which waited for: 6 -> 6; matrix products, arithmetic and copies ran while one was open for 8% -> 8% of each run, Pallas kernels for 0% -> 0%
where the time goes in v1:
time: 1060 us
  waiting for transfers between devices  762 us (72%)
  blocking collectives  158 us (15%)
  local copies, waits for them, and re-layouts  42.6 us (4%)
  other arithmetic  34.5 us (3%)
  matrix products  32.4 us (3%)
  between operations  15.2 us (1%)
  starting transfers between devices  12.4 us (1%)
    all_gather x1, waiting for transfers between devices, body(): lax.all_gather(attn_in.astype(jnp.bfloat16), ('rep', 'blk'), axis=0, tile...  310 us
    all_gather x1, waiting for transfers between devices, body(): lax.all_gather(attn_out.astype(jnp.bfloat16), ('rep', 'blk'), axis=0, til...  298 us
    all_gather x1, blocking collectives, body(): lax.all_gather(dense, 'blk', axis=0, tiled=True)  158 us
    reduce_scatter x1, waiting for transfers between devices, body(): lax.psum_scatter(summed.reshape(count * lax.axis_size('blk'), D).astype(j...  86.8 us
    all_gather x1, waiting for transfers between devices, body(): cache_all = lax.all_gather(cache_here, 'blk', axis=0, tiled=True)  42.1 us
    another operation x1, other arithmetic, slot_tables(): ranked = jnp.cumsum(member, axis=0) - 1  23.4 us
  transfers between devices with their start and end apart: 9, of which 6 were waited for; matrix products, arithmetic and copies ran while one was open for 8% of the time, Pallas kernels for 0%

profile of v1, /device:TPU:0, one launch (start us, length us, event | category | flops | bytes accessed | tf_op | source)
XLA Modules:
  0.0 1057.5 jit_solution(12842792803762128496)
XLA Ops:
  7.2 1.5 convert_bitcast_fusion
  8.8 1.5 convert_bitcast_fusion.1
  10.4 0.8 reduce-window_clone.1
  11.3 0.7 subtract_bitcast_fusion
  11.9 0.1 convert_reduce_fusion
  12.0 0.1 select_reduce_fusion.1
  12.1 0.1 dynamic-slice_convert_fusion
  12.2 0.2 multiply_cosine_fusion
  12.4 0.1 copy.89
  12.5 0.1 copy.90
  12.6 1.2 fusion.12
  13.8 310.3 %all-gather.14.cloned.1.call-done = bf16[128,12,2048]{2,1,0:T(8,128)(2,1)} async-done(((bf16[1,12,2048]{2,1,0:T(8,128)(2,1)}), bf16[128,12,2048]{2,1,0:T(8,128)(2,1)}) %all-gather.14.cloned.1.call-update) | async-done | bytes 6291472 | tf_op jit(solution)/shard_map/all_gather | solution.py:94
  324.1 10.7 %reshape.239 = bf16[1536,2048]{1,0:T(8,128)(2,1)} reshape(bf16[128,12,2048]{2,1,0:T(8,128)(2,1)} %all-gather.14.cloned.1.call-done) | data formatting | bytes 12582912
  334.8 3.8 fusion.28
  338.7 0.1 reshape.219
  338.7 0.3 subtract_convert_fusion.1
  339.0 0.2 pad_maximum_fusion.2
  339.2 0.7 pad_maximum_fusion.1
  340.0 0.1 dynamic_slice.10
  340.1 0.2 fusion.17
  340.3 297.7 %all-gather.16.cloned.1.call-done = bf16[128,12,1536]{2,1,0:T(8,128)(2,1)} async-done(((bf16[1,12,1536]{2,1,0:T(8,128)(2,1)}), bf16[128,12,1536]{2,1,0:T(8,128)(2,1)}) %all-gather.16.cloned.1.call-update) | async-done | bytes 4718608 | tf_op jit(solution)/shard_map/all_gather | solution.py:123
  637.9 8.2 reshape.241
  646.1 0.1 slice.53
  646.2 0.3 copy.91
  646.5 0.1 subtract_convert_fusion
  646.6 0.2 copy.92
  646.8 0.2 copy.93
  647.1 42.1 %all-gather.8.cloned.1.call-done = bf16[1024,512]{1,0:T(8,128)(2,1)} async-done(((bf16[128,512]{1,0:T(8,128)(2,1)}), bf16[1024,512]{1,0:T(8,128)(2,1)}) %all-gather.8.cloned.1.call-update) | async-done | bytes 1048592 | tf_op jit(solution)/shard_map/all_gather | solution.py:103
  689.2 1.3 fusion.49
  690.5 0.1 reshape.221
  690.6 0.2 copy.115
  690.8 4.8 fusion.50
  695.6 3.5 fusion.11
  699.2 0.4 slice-done.1
  699.6 0.9 multiply_reduce_fusion
  700.5 0.9 multiply_convert_fusion
  701.5 0.1 convert_element_type.95
  701.5 1.2 copy.102
  702.8 3.7 all-to-all-start
  706.6 0.9 copy.106
  707.5 16.5 %all-to-all-done = bf16[16,12,1536]{2,1,0:T(8,128)(2,1)S(1)} async-done(((bf16[16,12,1536]{2,1,0:T(8,128)(2,1)}), bf16[16,12,1536]{2,1,0:T(8,128)(2,1)S(1)}, u32[]{:S(2)}, u32[]{:S(2)}) %all-to-all-start) | async-done | bytes 589856 | tf_op jit(solution)/shard_map/all_to_all | solution.py:150
  724.0 3.5 all-to-all-start.2
  727.4 0.6 copy.103
  728.0 0.1 copy.104
  728.1 8.7 all-to-all-done.2
  736.8 4.7 stack.5
  741.6 4.9 all-to-all-start.1
  746.5 0.2 copy.107
  746.8 0.7 copy.108
  747.6 158.3 %all_gather.21 = bf16[1024,16]{0,1:T(8,128)(2,1)S(1)} all-gather(bf16[128,16]{0,1:T(8,128)(2,1)S(1)} %select_reduce_fusion), channel_id=1, replica_groups=mesh['rep'=16,'blk'=8] {'blk'}, dimensions={0}, use_global_device_ids=true | all-gather | bytes 36864 | tf_op jit(solution)/shard_map/all_gather | solution.py:159
  906.0 0.3 copy.98
  906.3 23.4 %add_bitcast_fusion = s32[2,8,128]{0,1,2:T(8,128)S(1)} fusion(s32[8,128,2]{2,0,1:T(8,128)S(1)} %copy.98), kind=kOutput, calls=%fused_computation.31 | output fusion | flops 262144 | bytes 16384 | tf_op jit(solution)/shard_map/vmap(jit(cumsum))/reduce_window_sum | solution.py:58
  929.7 0.2 copy.99
  929.9 8.3 copy.105
  938.2 3.0 fusion.2
  941.2 0.3 copy.101
  941.5 1.3 copy-done
  942.9 6.9 fusion.55
  949.7 6.8 convolution_convert_fusion
  956.6 2.7 bitcast_convert_fusion
  959.3 0.6 fusion.39
  960.6 1.5 gather_fusion
  962.1 86.8 %reduce-scatter.2.cloned.1.call-done = bf16[128,1536]{1,0:T(8,128)(2,1)} async-done(((bf16[1024,1536]{1,0:T(8,128)(2,1)}), bf16[128,1536]{1,0:T(8,128)(2,1)}) %reduce-scatter.2.cloned.1.call-update) | async-done | bytes 393232 | tf_op jit(solution)/shard_map/reduce_scatter | solution.py:188
  1048.9 1.8 add_convert_fusion
  (57 shorter events, 0.6 us)
Async XLA Ops:
  7.2 316.9 %all-gather.14.cloned.1.call-start = ((), (), s32[]{:S(2)}) async-start(), calls=%async_computation.8 | async-start | bytes 8454144 | tf_op jit(solution)/shard_map/all_gather | solution.py:94
  8.8 629.2 %all-gather.16.cloned.1.call-start = ((), (), s32[]{:S(2)}) async-start(), calls=%async_computation.9 | async-start | bytes 6340608 | tf_op jit(solution)/shard_map/all_gather | solution.py:123
  10.4 678.8 %all-gather.8.cloned.1.call-start = ((), (), s32[]{:S(2)}) async-start(), calls=%async_computation.4 | async-start | bytes 1179648 | tf_op jit(solution)/shard_map/all_gather | solution.py:103
  13.8 321.0 %copy-start.2 = (bf16[128,1536]{1,0:T(8,128)(2,1)S(1)}, bf16[128,1536]{1,0:T(8,128)(2,1)}, u32[]{:S(2)}) copy-start(bf16[128,1536]{1,0:T(8,128)(2,1)} %param.11) | copy-start | bytes 1179652
  13.8 321.0 %copy-start.5 = (f32[1536]{0:T(1024)S(1)}, f32[1536]{0:T(1024)}, u32[]{:S(2)}) copy-start(f32[1536]{0:T(1024)} %param.16) | copy-start | bytes 18436
  339.9 598.3 %all-gather.10.cloned.1.call-start = ((), (), s32[]{:S(2)}) async-start(), calls=%async_computation.5 | async-start | bytes 3538944 | tf_op jit(solution)/shard_map/all_gather | solution.py:158
  690.8 8.4 slice-start
  695.6 4.0 slice-start.1
  699.2 1.4 copy-start.6
  699.2 2.3 copy-start.3
  700.5 6.0 copy-start.4
  702.8 21.2 %all-to-all-start = ((bf16[16,12,1536]{2,1,0:T(8,128)(2,1)}), bf16[16,12,1536]{2,1,0:T(8,128)(2,1)S(1)}, u32[]{:S(2)}, u32[]{:S(2)}) async-start(bf16[16,12,1536]{2,1,0:T(8,128)(2,1)} %copy.102), calls=%async_computation | async-start | bytes 1572864 | tf_op jit(solution)/shard_map/all_to_all | solution.py:150
  724.0 12.9 %all-to-all-start.2 = ((bf16[16,6,1536]{2,1,0:T(8,128)(2,1)}), bf16[16,6,1536]{2,1,0:T(8,128)(2,1)S(1)}, u32[]{:S(2)}, u32[]{:S(2)}) async-start(bf16[16,6,1536]{2,1,0:T(8,128)(2,1)} %copy.106), calls=%async_computation.2 | async-start | bytes 786432 | tf_op jit(solution)/shard_map/all_to_all | solution.py:153
  741.6 6.0 copy-start.8
  741.6 6.1 copy-start.7
  741.6 188.4 %all-to-all-start.1 = ((bf16[16,2,96,1536]{3,2,1,0:T(8,128)(2,1)}), bf16[16,2,96,1536]{3,2,1,0:T(8,128)(2,1)}, u32[]{:S(2)}, u32[]{:S(2)}) async-start(bf16[16,2,96,1536]{3,2,1,0:T(8,128)(2,1)} %stack.5), calls=%async_computation.1 | async-start | bytes 18874368 | tf_op jit(solution)/shard_map/all_to_all | solution.py:22
  746.5 203.3 %all-gather.12.cloned.1.call-start = ((), (), s32[]{:S(2)}) async-start(), calls=%async_computation.6 | async-start | bytes 5013504 | tf_op jit(solution)/shard_map/all_gather | solution.py:182
  747.5 301.3 %reduce-scatter.2.cloned.1.call-start = ((), (), s32[]{:S(2)}) async-start(), calls=%async_computation.7 | async-start | bytes 3538944 | tf_op jit(solution)/shard_map/reduce_scatter | solution.py:188
  938.2 4.6 copy-start
  956.6 2.7 copy-start.9
  956.6 4.0 copy-start.1
Sparse Core Ops, SparseCore 0:
  10.3 313.7 all-gather.13
  326.3 311.5 all-gather.15
  640.9 48.2 all-gather.7
  701.6 72.3 all-gather.9
  776.0 103.3 all-gather.11
  959.4 89.4 reduce-scatter.1
